TPU v7x, 32 devices: a whole 2x2x4 slice. The times are simulated.
32 devices in a mesh: rep: 8 (over y, x, core), shard: 4 (over z).
Axes of the slice: x: 2, y: 2, z: 4, core: 2. Of those that a mesh axis runs over, the one named last changes fastest.
Arguments:
- tokens: bfloat16 [32, 512, 1024], P(('rep', 'shard')), may hold values from -6 to 6
- segments: int32 [32, 512], P(('rep', 'shard')), may hold values from 0 to 25, as said below
- lengths: int32 [32], P(('rep', 'shard')), may hold values from 449 to 512, as said below
- cotangent: bfloat16 [32, 512, 1024], P(('rep', 'shard')), may hold values from -6 to 6
- w_qkv: bfloat16 [1024, 3072], P('shard'), may hold values from -0.1875 to 0.1875
- b_qv: bfloat16 [2048], P('shard'), may hold values from -4 to 4
- w_out: bfloat16 [1024, 1024], P('shard'), may hold values from -0.5 to 0.5
- b_out: bfloat16 [1024], P('shard'), may hold values from -4 to 4
- gain_one: bfloat16 [1024], P('shard'), may hold values from 0.5 to 1.5
- shift_one: bfloat16 [1024], P('shard'), may hold values from -4 to 4
- w_in: bfloat16 [1024, 4096], P('shard'), may hold values from -0.1875 to 0.1875
- b_in: bfloat16 [4096], P('shard'), may hold values from -4 to 4
- w_down: bfloat16 [4096, 1024], P('shard'), may hold values from -0.09375 to 0.09375
- b_down: bfloat16 [1024], P('shard'), may hold values from -4 to 4
- gain_two: bfloat16 [1024], P('shard'), may hold values from 0.5 to 1.5
- shift_two: bfloat16 [1024], P('shard'), may hold values from -4 to 4
Outputs:
- layer_out: bfloat16 [32, 512, 1024], P(('rep', 'shard'))
- grad_tokens: float32 [32, 512, 1024], P(('rep', 'shard'))
- grad_w_qkv: float32 [1024, 3072], P('shard')
- grad_b_qv: float32 [2048], P('shard')
- grad_w_out: float32 [1024, 1024], P('shard')
- grad_b_out: float32 [1024], P('shard')
- grad_gain_one: float32 [1024], P('shard')
- grad_shift_one: float32 [1024], P('shard')
- grad_w_in: float32 [1024, 4096], P('shard')
- grad_b_in: float32 [4096], P('shard')
- grad_w_down: float32 [4096, 1024], P('shard')
- grad_b_down: float32 [1024], P('shard')
- grad_gain_two: float32 [1024], P('shard')
- grad_shift_two: float32 [1024], P('shard')
Inputs may be any that keep to these rules, and one draw needn't show every extreme that they name: `segments`: within a sequence the document numbers start at 0 and never fall; every document spans 20 to 200 positions unless the sequence's end cuts it; the first sequence is made of documents of 20 positions. `lengths`: positions from a sequence's length on are padding; the first sequence has none, the second has the most.
All inputs are finite; a program needn't handle non-finite values.
Results may differ from a plain program's by a relative error of at most 0.019.
Values may be sent and summed in bfloat16 or wider, within the bound.
No kernel may reach another device: no remote copies, remote signals or barrier semaphores. Data moves between devices by JAX's collectives and lax.ppermute only.
A program may use at most 192 MiB of HBM per device.

v0:
```python
from functools import partial
import jax
import jax.numpy as jnp
from jax import lax
from jax.sharding import Mesh
from jax.sharding import PartitionSpec as P

HEAD_DIM = 64
REP = ("chip", "core")
ALL = ("chip", "core", "shard")


def layer_norm(hidden, norm_gain, norm_shift):
    average = jnp.mean(hidden, axis=-1, keepdims=True)
    centred = hidden - average
    variance = jnp.mean(centred * centred, axis=-1, keepdims=True)
    return centred * lax.rsqrt(variance + 1e-06) * norm_gain + norm_shift


def matmul(left, right):
    return jnp.dot(left, right, preferred_element_type=jnp.float32)


def project_back(left, right):
    return lax.dot_general(
        left, right, (((1,), (1,)), ((), ())), preferred_element_type=jnp.float32
    )


def outer_sum(left, right):
    return lax.dot_general(
        left, right, (((0,), (0,)), ((), ())), preferred_element_type=jnp.float32
    )


def column_sum(values):
    return jnp.sum(values.astype(jnp.float32), axis=0)


def allowed_pairs(doc_ids, length):
    positions = jnp.arange(doc_ids.shape[0])
    is_valid = positions < length
    return (doc_ids[:, None] == doc_ids[None, :]) & (is_valid[:, None] == is_valid[None, :])


def attend(query_heads, key_heads, value_heads, allowed):
    scale = HEAD_DIM ** (-0.5)
    scores = (
        jnp.einsum("qhd,khd->hqk", query_heads, key_heads, preferred_element_type=jnp.float32)
        * scale
    )
    scores = jnp.where(allowed[None], scores, -1e30)
    maxima = jnp.max(scores, axis=2, keepdims=True)
    expo = jnp.exp(scores - maxima)
    totals = jnp.sum(expo, axis=2, keepdims=True)
    attn_probs = (expo / totals).astype(jnp.bfloat16)
    context = jnp.einsum(
        "hqk,khd->qhd", attn_probs, value_heads, preferred_element_type=jnp.float32
    )
    return (context.astype(jnp.bfloat16), maxima + jnp.log(totals))


def attend_back(query_heads, key_heads, value_heads, grad_context, allowed, log_totals):
    scale = HEAD_DIM ** (-0.5)
    scores = (
        jnp.einsum("qhd,khd->hqk", query_heads, key_heads, preferred_element_type=jnp.float32)
        * scale
    )
    scores = jnp.where(allowed[None], scores, -1e30)
    attn_probs = jnp.exp(scores - log_totals)
    grad_probs = jnp.einsum(
        "qhd,khd->hqk", grad_context, value_heads, preferred_element_type=jnp.float32
    )
    grad_scores = attn_probs * (
        grad_probs - jnp.sum(attn_probs * grad_probs, axis=2, keepdims=True)
    )
    grad_low = grad_scores.astype(jnp.bfloat16)
    grad_query = (
        jnp.einsum("hqk,khd->qhd", grad_low, key_heads, preferred_element_type=jnp.float32) * scale
    )
    grad_key = (
        jnp.einsum("hqk,qhd->khd", grad_low, query_heads, preferred_element_type=jnp.float32)
        * scale
    )
    grad_value = jnp.einsum(
        "hqk,qhd->khd",
        attn_probs.astype(jnp.bfloat16),
        grad_context,
        preferred_element_type=jnp.float32,
    )
    return (
        grad_query.astype(jnp.bfloat16),
        grad_key.astype(jnp.bfloat16),
        grad_value.astype(jnp.bfloat16),
    )


def local(
    chips,
    group,
    tokens,
    segments,
    lengths,
    cotangent,
    w_qkv,
    b_qv,
    w_out,
    b_out,
    gain_one,
    shift_one,
    w_in,
    b_in,
    w_down,
    b_down,
    gain_two,
    shift_two,
):
    reps = 2 * chips
    core = lax.axis_index("core")
    rank = lax.axis_index("chip") * 2 + core
    own = lax.axis_index("shard")
    _, seq_len, model_width = tokens.shape
    num_heads = model_width // HEAD_DIM
    split_shape = (seq_len, num_heads, HEAD_DIM)
    ff_rows = w_down.shape[0]
    ff_width = w_in.shape[1]
    qkv_width = w_qkv.shape[1]

    def from_shard(value, step):
        return lax.ppermute(value, "shard", [(i, (i - step) % group) for i in range(group)])

    def to_shard(value, step):
        return lax.ppermute(value, "shard", [(i, (i + step) % group) for i in range(group)])

    def sibling(value):
        return lax.ppermute(value, "core", [(0, 1), (1, 0)])

    def roll_left(value, width):
        twice = jnp.concatenate([value, value], axis=1)
        return lax.dynamic_slice_in_dim(twice, own * width, value.shape[1], axis=1)

    def roll_right(value, width):
        twice = jnp.concatenate([value, value], axis=1)
        start = (group - own) % group * width
        return lax.dynamic_slice_in_dim(twice, start, value.shape[1], axis=1)

    vectors = (b_qv, b_out, gain_one, shift_one, b_in, b_down, gain_two, shift_two)
    sizes = [v.shape[0] for v in vectors]
    w_one = jnp.concatenate([w_qkv, w_out], axis=1)
    part = w_one.shape[1] // reps
    rows = w_one.shape[0]
    packed = jnp.concatenate(vectors)
    extra = -(-packed.shape[0] // (16 * part)) * 16
    packed = jnp.pad(packed, (0, extra * part - packed.shape[0])).reshape(extra, part)
    piece_one = jnp.concatenate(
        [lax.dynamic_slice_in_dim(w_one, rank * part, part, axis=1), packed], axis=0
    )
    part_in = ff_width // reps
    piece_in = lax.dynamic_slice_in_dim(w_in, rank * part_in, part_in, axis=1)
    part_down = ff_rows // reps
    piece_down = lax.dynamic_slice_in_dim(w_down, rank * part_down, part_down, axis=0)
    got_one = [from_shard(piece_one, s) for s in range(1, group)]
    got_in = [from_shard(piece_in, s) for s in range(1, group)]
    got_down = [from_shard(piece_down, s) for s in range(1, group)]
    rest_one = lax.all_gather(
        jnp.concatenate([g[:rows] for g in got_one], axis=0), REP, axis=1, tiled=True
    )
    rest_in = lax.all_gather(jnp.concatenate(got_in, axis=0), REP, axis=1, tiled=True)
    rest_down = lax.all_gather(jnp.stack(got_down), REP, axis=1, tiled=True)
    rest_down = rest_down.reshape(-1, model_width)
    relative = jnp.stack([packed.reshape(-1)] + [g[rows:].reshape(-1) for g in got_one])
    natural = jnp.concatenate([relative, relative], axis=0)
    natural = lax.dynamic_slice_in_dim(natural, (group - own) % group, group, axis=0)
    full, start = ([], 0)
    for size in sizes:
        full.append(natural[:, start : start + size].reshape(-1).astype(jnp.float32))
        start += size
    bias_qv, bias_out, norm_gone, norm_sone, bias_in, bias_down, norm_gtwo, norm_stwo = full
    own_qkv, own_out = (w_qkv, w_out)
    rest_qkv, rest_out = (rest_one[:, :qkv_width], rest_one[:, qkv_width:])
    flat_in = tokens[0]
    in_rel = roll_left(flat_in, rows)
    projected = matmul(in_rel[:, :rows], own_qkv) + matmul(in_rel[:, rows:], rest_qkv)
    queries = (projected[:, :model_width] + bias_qv[:model_width]).astype(jnp.bfloat16)
    key_rows = projected[:, model_width : 2 * model_width].astype(jnp.bfloat16)
    value_rows = (projected[:, 2 * model_width :] + bias_qv[model_width:]).astype(jnp.bfloat16)
    query_heads = queries.reshape(split_shape)
    key_heads = key_rows.reshape(split_shape)
    value_heads = value_rows.reshape(split_shape)
    allowed = allowed_pairs(segments[0], lengths[0])
    context, log_totals = attend(query_heads, key_heads, value_heads, allowed)
    context_rel = roll_left(context.reshape(-1, model_width), rows)
    attn_out = (
        matmul(context_rel[:, :rows], own_out) + matmul(context_rel[:, rows:], rest_out) + bias_out
    )
    first_sum = flat_in.astype(jnp.float32) + attn_out
    normed_one = layer_norm(first_sum, norm_gone, norm_sone)
    normed_rel = roll_left(normed_one.astype(jnp.bfloat16), rows)
    inner = matmul(normed_rel[:, :rows], w_in) + matmul(normed_rel[:, rows:], rest_in) + bias_in
    activated = jax.nn.gelu(inner, approximate=False)
    act_rel = roll_left(activated.astype(jnp.bfloat16), ff_rows)
    branch = (
        matmul(act_rel[:, :ff_rows], w_down) + matmul(act_rel[:, ff_rows:], rest_down) + bias_down
    )
    second_sum = normed_one + branch
    output_rows = layer_norm(second_sum, norm_gtwo, norm_stwo)

    def half(value, width, which):
        split = value.reshape(seq_len, -1, 2, width)
        return lax.dynamic_index_in_dim(split, which, axis=2, keepdims=False).reshape(seq_len, -1)

    def pair(value, width):
        return (half(value, width, core), sibling(half(value, width, 1 - core)))

    def both(left, right):
        return outer_sum(left[0], right[0]) + outer_sum(left[1], right[1])

    in_pair = (in_rel, sibling(in_rel))
    context_pair = (context_rel, sibling(context_rel))
    normed_pair = (normed_rel, sibling(normed_rel))
    act_pair = pair(act_rel, part_down)

    def own_sum(parts):
        total = parts[0].astype(jnp.float32)
        for s in range(1, group):
            total = total + to_shard(parts[s], s).astype(jnp.float32)
        return total.astype(jnp.bfloat16)

    def scatter_columns(grad):
        share = lax.psum_scatter(grad.astype(jnp.bfloat16), "chip", scatter_dimension=1, tiled=True)
        share = own_sum(share.reshape(group, rows, -1))
        return lax.all_gather(share, REP, axis=1, tiled=True).astype(jnp.float32)

    grad_rows = cotangent[0].astype(jnp.float32)
    _, norm_two_back = jax.vjp(layer_norm, second_sum, norm_gtwo, norm_stwo)
    grad_second, grad_gtwo, grad_stwo = norm_two_back(grad_rows)
    grad_branch = grad_second.astype(jnp.bfloat16)
    branch_pair = (grad_branch, sibling(grad_branch))
    grad_bdown = column_sum(grad_branch)
    grad_down = both(act_pair, branch_pair).astype(jnp.bfloat16)
    grad_down = lax.psum_scatter(
        grad_down.reshape(group, chips * part_down, model_width),
        "chip",
        scatter_dimension=1,
        tiled=True,
    )
    grad_wdown = lax.all_gather(own_sum(grad_down), REP, axis=0, tiled=True).astype(jnp.float32)
    grad_act = jnp.concatenate(
        [project_back(grad_branch, w_down), project_back(grad_branch, rest_down)], axis=1
    )
    grad_act = roll_right(grad_act, ff_rows)
    _, gelu_back = jax.vjp(partial(jax.nn.gelu, approximate=False), inner)
    grad_inner = gelu_back(grad_act)[0].astype(jnp.bfloat16)
    grad_win = scatter_columns(both(normed_pair, pair(grad_inner, part_in)))
    grad_bin = column_sum(grad_inner)
    back_in = jnp.concatenate(
        [project_back(grad_inner, w_in), project_back(grad_inner, rest_in)], axis=1
    )
    grad_normed = grad_second + roll_right(back_in, rows)
    _, norm_one_back = jax.vjp(layer_norm, first_sum, norm_gone, norm_sone)
    grad_first, grad_gone, grad_sone = norm_one_back(grad_normed)
    grad_attn = grad_first.astype(jnp.bfloat16)
    half_out = both(context_pair, pair(grad_attn, part))
    grad_bout = column_sum(grad_attn)
    grad_context = jnp.concatenate(
        [project_back(grad_attn, own_out), project_back(grad_attn, rest_out)], axis=1
    ).astype(jnp.bfloat16)
    grad_context = roll_right(grad_context, rows).reshape(split_shape)
    grad_query, grad_key, grad_value = attend_back(
        query_heads, key_heads, value_heads, grad_context, allowed, log_totals
    )
    grad_query = grad_query.reshape(-1, model_width)
    grad_key = grad_key.reshape(-1, model_width)
    grad_value = grad_value.reshape(-1, model_width)
    grad_proj = jnp.concatenate([grad_query, grad_key, grad_value], axis=1)
    half_qkv = both(in_pair, pair(grad_proj, part))
    grad_one = scatter_columns(jnp.concatenate([half_qkv, half_out], axis=1))
    back_proj = jnp.concatenate(
        [project_back(grad_proj, own_qkv), project_back(grad_proj, rest_qkv)], axis=1
    )
    grad_input = grad_first + roll_right(back_proj, rows)
    small = (
        jnp.concatenate([column_sum(grad_query), column_sum(grad_value)]),
        grad_bout,
        grad_gone,
        grad_sone,
        grad_bin,
        grad_bdown,
        grad_gtwo,
        grad_stwo,
    )
    small = jnp.concatenate([v.reshape(group, -1) for v in small], axis=1)
    small = lax.psum(small, ALL)
    small = lax.dynamic_index_in_dim(small, own, axis=0, keepdims=False)
    vecs, start = ([], 0)
    for size in sizes:
        vecs.append(small[start : start + size])
        start += size
    return (
        output_rows.astype(jnp.bfloat16).reshape(tokens.shape),
        grad_input.reshape(tokens.shape),
        grad_one[:, :qkv_width],
        vecs[0],
        grad_one[:, qkv_width:],
        vecs[1],
        vecs[2],
        vecs[3],
        grad_win,
        vecs[4],
        grad_wdown,
        vecs[5],
        vecs[6],
        vecs[7],
    )


def solution(mesh):
    reps, group = mesh.devices.shape
    fine = Mesh(mesh.devices.reshape(reps // 2, 2, group), ALL)
    rows = P(ALL, None, None)
    matrix = P("shard", None)
    vector = P("shard")
    in_specs = (
        rows,
        P(ALL, None),
        P(ALL),
        rows,
        matrix,
        vector,
        matrix,
        vector,
        vector,
        vector,
        matrix,
        vector,
        matrix,
        vector,
        vector,
        vector,
    )
    out_specs = (
        rows,
        rows,
        matrix,
        vector,
        matrix,
        vector,
        vector,
        vector,
        matrix,
        vector,
        matrix,
        vector,
        vector,
        vector,
    )
    return jax.shard_map(
        partial(local, reps // 2, group),
        mesh=fine,
        in_specs=in_specs,
        out_specs=out_specs,
        check_vma=False,
    )
```

profile of v0, /device:TPU:0, one launch (start us, length us, event | category | flops | bytes accessed | tf_op | source)
XLA Modules:
  0.0 575.3 jit_solution(13355373292585005239)
XLA Ops:
  15.2 3.1 collective-permute-start.2
  22.3 5.7 collective-permute-done.2
  28.0 11.1 %collective-permute-done.1 = bf16[272,512]{1,0:T(8,128)(2,1)S(1)} collective-permute-done((bf16[272,512]{1,0:T(8,128)(2,1)S(1)}, bf16[272,512]{1,0:T(8,128)(2,1)S(1)}, u32[]{:S(2)}, u32[]{:S(2)}) %collective-permute-start.1) | collective-permute-done | bytes 278560 | tf_op jit(solution)/shard_map/ppermute | solution.py:130
  41.6 5.8 %collective-permute-start.5 = (bf16[256,512]{1,0:T(8,128)(2,1)S(1)}, bf16[256,512]{1,0:T(8,128)(2,1)S(1)}, u32[]{:S(2)}, u32[]{:S(2)}) collective-permute-start(bf16[256,512]{1,0:T(8,128)(2,1)S(1)} %constant_dynamic-slice_fusion.11), channel_id=1, source_target_pairs={{0,1},{1,2},{2,3},{3,0},{4,5},{5,6},{6,7},{7,4},{8,9},{9,10},{10,1... | collective-permute-start | bytes 786440 | tf_op jit(solution)/shard_map/ppermute | solution.py:130
  49.8 6.6 %collective-permute-done.5 = bf16[256,512]{1,0:T(8,128)(2,1)S(1)} collective-permute-done((bf16[256,512]{1,0:T(8,128)(2,1)S(1)}, bf16[256,512]{1,0:T(8,128)(2,1)S(1)}, u32[]{:S(2)}, u32[]{:S(2)}) %collective-permute-start.5) | collective-permute-done | bytes 262176 | tf_op jit(solution)/shard_map/ppermute | solution.py:130
  56.4 9.4 %collective-permute-done.4 = bf16[256,512]{1,0:T(8,128)(2,1)S(1)} collective-permute-done((bf16[256,512]{1,0:T(8,128)(2,1)S(1)}, bf16[256,512]{1,0:T(8,128)(2,1)S(1)}, u32[]{:S(2)}, u32[]{:S(2)}) %collective-permute-start.4) | collective-permute-done | bytes 262176 | tf_op jit(solution)/shard_map/ppermute | solution.py:130
  68.6 6.1 %collective-permute-start.8 = (bf16[128,1024]{1,0:T(8,128)(2,1)}, bf16[128,1024]{1,0:T(8,128)(2,1)}, u32[]{:S(2)}, u32[]{:S(2)}) collective-permute-start(bf16[128,1024]{1,0:T(8,128)(2,1)} %constant_dynamic-slice_fusion.10), channel_id=1, source_target_pairs={{0,1},{1,2},{2,3},{3,0},{4,5},{5,6},{6,7},{7,4},{8,9},{9,10},{10,1... | collective-permute-start | bytes 786440 | tf_op jit(solution)/shard_map/ppermute | solution.py:130
  79.7 3.7 collective-permute-done.8
  83.4 10.0 %collective-permute-done.7 = bf16[128,1024]{1,0:T(8,128)(2,1)} collective-permute-done((bf16[128,1024]{1,0:T(8,128)(2,1)}, bf16[128,1024]{1,0:T(8,128)(2,1)}, u32[]{:S(2)}, u32[]{:S(2)}) %collective-permute-start.7) | collective-permute-done | bytes 262176 | tf_op jit(solution)/shard_map/ppermute | solution.py:130
  100.2 4.8 fusion.18
  114.8 9.4 %fusion.82 = (f32[16,512]{1,0:T(8,128)S(1)}, f32[16,512,512]{1,2,0:T(8,128)}) fusion(bf16[512,16,64]{0,2,1:T(8,128)(2,1)} %bitcast.174, bf16[512,16,64]{0,2,1:T(8,128)(2,1)S(1)} %bitcast.172, pred[512,512]{0,1:T(8,128)(4,1)S(1)} %compare_and_fusion), kind=kOutput, calls=%fused_computation.211 | convolution fusion | flops 549445632 | bytes 19169280 | tf_op jit(solution)/shard_map/qhd,khd->hqk/dot_general | solution.py:49
  124.3 8.4 %fusion = f32[16,512]{1,0:T(8,128)S(1)} fusion(f32[16,512,512]{1,2,0:T(8,128)} %get-tuple-element.65, f32[16,512]{1,0:T(8,128)S(1)} %get-tuple-element.64), kind=kLoop, calls=%fused_computation.10 | loop fusion | flops 8380416 | bytes 16842752 | tf_op jit(solution)/shard_map/reduce_sum | solution.py:55
  132.6 7.7 %fusion.42 = bf16[16,64,512]{2,1,0:T(8,128)(2,1)S(1)} fusion(bf16[512,16,64]{0,2,1:T(8,128)(2,1)S(1)} %bitcast.184, f32[16,512,512]{1,2,0:T(8,128)} %get-tuple-element.65, f32[16,512]{1,0:T(8,128)S(1)} %fusion, f32[16,512]{1,0:T(8,128)S(1)} %get-tuple-element.64), kind=kOutput, calls=%fused_computation.115 | convolution fusion | flops 549978112 | bytes 18939904 | tf_op jit(solution)/shard_map/hqk,khd->qhd/dot_general | solution.py:57
  149.9 4.6 fusion.67
  154.5 24.8 %multiply_convert_fusion.1 = (bf16[512,4096]{1,0:T(8,128)(2,1)S(1)}, f32[512,4096]{1,0:T(8,128)}) fusion(f32[4096]{0:T(1024)S(1)} %bitcast.218, f32[512,4096]{1,0:T(8,128)} %fusion.67, bf16[768,4096]{1,0:T(8,128)(2,1)} %all-gather.9.cloned.1.call-done, bf16[512,1024]{1,0:T(8,128)(2,1)S(1)} %fusion.54), kind=kOutput, calls=%fused_computation.25 | convolution fusion | flops 3361734656 | bytes 28065792 | tf_op jit(solution)/shard_map/dot_general | solution.py:21
  186.3 3.7 all-gather.11.cloned.1.call-done
  190.0 8.7 %fusion.84 = (f32[512]{0:T(512)S(1)}, f32[512,1024]{1,0:T(8,128)S(1)}) fusion(f32[1024]{0:T(1024)S(1)} %bitcast.220, f32[512,1024]{1,0:T(8,128)} %fusion.57, bf16[3072,1024]{1,0:T(8,128)(2,1)} %bitcast.229, bf16[512,4096]{1,0:T(8,128)(2,1)} %copy-done.6, f32[1024]{0:T(1024)S(1)} %bitcast.214, f32[1024]{0:T(1024)S(1)} %bitcast.207, f32[512]{0:T(512)S(1)} %fusion.72, ...), kind=kOutput, calls=%fused_computation.213 | convolution fusion | flops 3225419264 | bytes 15747072 | tf_op jit(solution)/shard_map/dot_general | solution.py:21
  202.2 6.1 %fusion.86 = f32[512,3072]{1,0:T(8,128)S(1)} fusion(bf16[512,1024]{1,0:T(8,128)(2,1)S(1)} %get-tuple-element.20, bf16[3072,1024]{1,0:T(8,128)(2,1)} %bitcast.230), kind=kOutput, calls=%fused_computation.215 | convolution fusion | flops 3221225472 | bytes 13631488 | tf_op jit(solution)/shard_map/dot_general | solution.py:25
  209.7 23.1 %convert_reduce_fusion = (f32[4096]{0:T(1024)S(1)}, bf16[512,4096]{1,0:T(8,128)(2,1)S(1)}) fusion(f32[512,4096]{1,0:T(8,128)S(1)} %bitcast.179, s32[]{:T(128)S(6)} %select_n.73, f32[512,3072]{1,0:T(8,128)S(1)} %fusion.86, f32[512,1024]{1,0:T(8,128)S(1)} %fusion.85), kind=kLoop, calls=%fused_computation.22 | loop fusion | flops 161476608 | bytes 20987908 | tf_op jit(solution)/shard_map/reduce_sum | solution.py:37
  234.3 5.9 %fusion.88 = f32[512,768]{1,0:T(8,128)S(1)} fusion(bf16[512,4096]{1,0:T(8,128)(2,1)S(1)} %get-tuple-element.22, bf16[768,4096]{1,0:T(8,128)(2,1)} %all-gather.9.cloned.1.call-done), kind=kOutput, calls=%fused_computation.217 | convolution fusion | flops 3221225472 | bytes 12058624 | tf_op jit(solution)/shard_map/dot_general | solution.py:25
  248.7 8.6 %convert_reduce_fusion.4 = (f32[16,64]{1,0:T(8,128)S(1)}, bf16[16,64,512]{2,1,0:T(8,128)(2,1)S(1)}) fusion(bf16[512,16,64]{0,2,1:T(8,128)(2,1)S(1)} %bitcast.176, f32[16,512,512]{1,2,0:T(8,128)} %get-tuple-element.65, f32[16,512]{1,0:T(8,128)S(1)} %log_add_fusion), kind=kOutput, calls=%fused_computation.100 | convolution fusion | flops 546831360 | bytes 18911232 | tf_op jit(solution)/shard_map/hqk,qhd->khd/dot_general | solution.py:85
  257.4 11.4 %multiply_reduce_fusion = (f32[16,512]{1,0:T(8,128)S(1)}, f32[16,512,512]{1,2,0:T(8,128)}) fusion(f32[16,512,512]{1,2,0:T(8,128)} %get-tuple-element.65, f32[16,512]{1,0:T(8,128)S(1)} %log_add_fusion, bf16[512,16,64]{0,2,1:T(8,128)(2,1)S(1)} %bitcast.177, bf16[512,16,64]{0,2,1:T(8,128)(2,1)S(1)} %bitcast.185), kind=kOutput, calls=%fused_computation.5 | convolution fusion | flops 549445632 | bytes 35717120 | tf_op jit(solution)/shard_map/qhd,khd->hqk/dot_general | solution.py:71
  268.8 12.0 %multiply_convert_fusion = bf16[16,512,512]{1,2,0:T(8,128)(2,1)S(1)} fusion(f32[16,512,512]{1,2,0:T(8,128)} %get-tuple-element.73, f32[16,512,512]{1,2,0:T(8,128)} %get-tuple-element.65, f32[16,512]{1,0:T(8,128)S(1)} %get-tuple-element.72, f32[16,512]{1,0:T(8,128)S(1)} %log_add_fusion), kind=kLoop, calls=%fused_computation.4 | loop fusion | flops 16777216 | bytes 42008576 | tf_op jit(solution)/shard_map/convert_element_type | solution.py:77
  299.6 3.6 add_convert_fusion.3
  306.0 8.1 %reshape.403 = bf16[512,4,2,512]{3,2,1,0:T(2,128)(2,1)} reshape(bf16[512,4096]{1,0:T(8,128)(2,1)} %copy-done.7) | data formatting | bytes 8388608 | tf_op jit(solution)/shard_map/reshape | solution.py:209
  314.0 11.3 %constant_dynamic-slice_fusion.3 = (bf16[512,4,1,512]{3,2,1,0:T(2,128)(2,1)}, bf16[512,4,1,512]{3,2,1,0:T(2,128)(2,1)}) fusion(bf16[512,4,2,512]{3,2,1,0:T(2,128)(2,1)} %reshape.403, s32[]{:T(128)S(6)} %select_n.76, s32[]{:T(128)S(6)} %select_n.75), kind=kLoop, calls=%fused_computation.175 | loop fusion | bytes 8388616 | tf_op jit(solution)/shard_map/jit(dynamic_index_in_dim)/dynamic_slice | solution.py:210
  325.3 9.1 %copy.100 = bf16[512,4,1,512]{0,3,1,2:T(8,128)(2,1)S(1)} copy(bf16[512,4,1,512]{3,2,1,0:T(2,128)(2,1)} %get-tuple-element.34) | data formatting | bytes 4194304
  334.9 10.5 %copy.99 = bf16[512,4,1,512]{0,3,1,2:T(8,128)(2,1)} copy(bf16[512,4,1,512]{3,2,1,0:T(2,128)(2,1)} %get-tuple-element.35) | data formatting | bytes 4194304
  345.5 4.3 fusion.90
  349.8 6.3 %add_convert_fusion.1 = bf16[1024,2048]{1,0:T(8,128)(2,1)} fusion(f32[1024,2048]{1,0:T(8,128)S(1)} %fusion.90, bf16[512,1024]{1,0:T(8,128)(2,1)} %collective-permute-done.16, bf16[512,2048]{0,1:T(8,128)(2,1)} %collective-permute-done.17), kind=kOutput, calls=%fused_computation.21 | convolution fusion | flops 2151677952 | bytes 15728640 | tf_op jit(solution)/shard_map/dot_general | solution.py:31
  356.2 6.5 %copy.88 = bf16[512,4096]{0,1:T(8,128)(2,1)} copy(bf16[512,4096]{1,0:T(8,128)(2,1)} %copy-done.6) | data formatting | bytes 8388608 | tf_op jit(solution)/shard_map/dynamic_slice | solution.py:140
  371.1 4.5 add_convert_fusion
  376.9 3.8 collective-permute-start.15
  381.8 5.7 collective-permute-done.15
  387.5 16.6 %collective-permute-done.14 = bf16[256,512]{1,0:T(8,128)(2,1)S(1)} collective-permute-done((bf16[256,512]{1,0:T(8,128)(2,1)S(1)}, bf16[256,512]{1,0:T(8,128)(2,1)S(1)}, u32[]{:S(2)}, u32[]{:S(2)}) %collective-permute-start.14) | collective-permute-done | bytes 262176 | tf_op jit(solution)/shard_map/ppermute | solution.py:133
  405.9 9.9 %reduce-scatter.6.cloned.1.call-done = bf16[1024,512]{1,0:T(8,128)(2,1)} async-done(((bf16[1024,2048]{1,0:T(8,128)(2,1)}), bf16[1024,512]{1,0:T(8,128)(2,1)}) %reduce-scatter.6.cloned.1.call-update) | async-done | bytes 1048592 | tf_op jit(solution)/shard_map/reduce_scatter | solution.py:230
  417.0 3.4 collective-permute-start.20
  421.5 5.7 collective-permute-done.20
  427.2 15.7 %collective-permute-done.19 = bf16[256,512]{1,0:T(8,128)(2,1)S(1)} collective-permute-done((bf16[256,512]{1,0:T(8,128)(2,1)S(1)}, bf16[256,512]{1,0:T(8,128)(2,1)S(1)}, u32[]{:S(2)}, u32[]{:S(2)}) %collective-permute-start.19) | collective-permute-done | bytes 262176 | tf_op jit(solution)/shard_map/ppermute | solution.py:133
  444.8 27.2 %reduce-scatter.8.cloned.1.call-done = bf16[4,128,1024]{2,1,0:T(8,128)(2,1)} async-done(((bf16[4,512,1024]{2,1,0:T(8,128)(2,1)}), bf16[4,128,1024]{2,1,0:T(8,128)(2,1)}) %reduce-scatter.8.cloned.1.call-update) | async-done | bytes 1048592 | tf_op jit(solution)/shard_map/reduce_scatter | solution.py:241
  473.2 3.4 collective-permute-start.25
  477.7 5.6 collective-permute-done.25
  483.3 15.8 %collective-permute-done.24 = bf16[128,1024]{1,0:T(8,128)(2,1)S(1)} collective-permute-done((bf16[128,1024]{1,0:T(8,128)(2,1)S(1)}, bf16[128,1024]{1,0:T(8,128)(2,1)S(1)}, u32[]{:S(2)}, u32[]{:S(2)}) %collective-permute-start.24) | collective-permute-done | bytes 262176 | tf_op jit(solution)/shard_map/ppermute | solution.py:133
  501.4 40.2 %psum.7 = f32[4,3072]{1,0:T(4,128)S(1)} all-reduce(f32[4,3072]{1,0:T(4,128)S(1)} %constant_dynamic-update-slice_fusion), channel_id=1, replica_groups=mesh['chip'=4,'core'=2,'shard'=4] {'chip','core','shard'}, use_global_device_ids=true, to_apply=%region_21.22 | all-reduce | flops 12288 | bytes 98304 | tf_op jit(solution)/shard_map/psum | solution.py:293
  546.6 5.1 fusion.16
  553.7 3.6 slice.278
  558.4 4.3 convert_element_type.279
  564.4 4.1 convert_element_type.287
  (270 shorter events, 124.4 us)
Async XLA Ops:
  7.2 34.3 %copy-start = (bf16[256,4096]{1,0:T(8,128)(2,1)S(1)}, bf16[256,4096]{1,0:T(8,128)(2,1)}, u32[]{:S(2)}) copy-start(bf16[256,4096]{1,0:T(8,128)(2,1)} %param.26) | copy-start | bytes 6291460
  7.2 93.0 %all-gather.7.cloned.1.call-start = ((), (), s32[]{:S(2)}) async-start(), calls=%async_computation.3 | async-start | bytes 7077888 | tf_op jit(solution)/shard_map/all_gather | solution.py:165
  15.2 62.5 %copy-start.17 = (bf16[1,512,1024]{2,1,0:T(8,128)(2,1)S(1)}, bf16[1,512,1024]{2,1,0:T(8,128)(2,1)}, u32[]{:S(2)}) copy-start(bf16[1,512,1024]{2,1,0:T(8,128)(2,1)} %param.16) | copy-start | bytes 3145732
  15.2 12.7 %collective-permute-start.2 = (bf16[272,512]{1,0:T(8,128)(2,1)S(1)}, bf16[272,512]{1,0:T(8,128)(2,1)S(1)}, u32[]{:S(2)}, u32[]{:S(2)}) collective-permute-start(bf16[272,512]{1,0:T(8,128)(2,1)S(1)} %pad_maximum_fusion.8), channel_id=1, source_target_pairs={{0,1},{1,2},{2,3},{3,0},{4,5},{5,6},{6,7},{7,4},{8,9},{9,10},{10,1... | collective-permute-start | bytes 835592 | tf_op jit(solution)/shard_map/ppermute | solution.py:130
  18.3 20.8 %collective-permute-start.1 = (bf16[272,512]{1,0:T(8,128)(2,1)S(1)}, bf16[272,512]{1,0:T(8,128)(2,1)S(1)}, u32[]{:S(2)}, u32[]{:S(2)}) collective-permute-start(bf16[272,512]{1,0:T(8,128)(2,1)S(1)} %pad_maximum_fusion.8), channel_id=1, source_target_pairs={{0,2},{1,3},{2,0},{3,1},{4,6},{5,7},{6,4},{7,5},{8,10},{9,11},{10,... | collective-permute-start | bytes 835592 | tf_op jit(solution)/shard_map/ppermute | solution.py:130
  20.9 18.2 %collective-permute-start = (bf16[272,512]{1,0:T(8,128)(2,1)S(1)}, bf16[272,512]{1,0:T(8,128)(2,1)S(1)}, u32[]{:S(2)}, u32[]{:S(2)}) collective-permute-start(bf16[272,512]{1,0:T(8,128)(2,1)S(1)} %pad_maximum_fusion.8), channel_id=1, source_target_pairs={{0,3},{1,0},{2,1},{3,2},{4,7},{5,4},{6,5},{7,6},{8,11},{9,8},{10,9... | collective-permute-start | bytes 835592 | tf_op jit(solution)/shard_map/ppermute | solution.py:130
  28.0 11.1 %copy-start.33 = (bf16[272,512]{1,0:T(8,128)(2,1)}, bf16[272,512]{1,0:T(8,128)(2,1)S(1)}, u32[]{:S(2)}) copy-start(bf16[272,512]{1,0:T(8,128)(2,1)S(1)} %collective-permute-done.2) | copy-start | bytes 835588
  39.1 40.3 %copy-start.40 = (s32[1,512]{1,0:T(1,128)S(1)}, s32[1,512]{1,0:T(1,128)}, u32[]{:S(2)}) copy-start(s32[1,512]{1,0:T(1,128)} %param.17) | copy-start | bytes 6148
  41.5 113.0 %all-gather.9.cloned.1.call-start = ((), (), s32[]{:S(2)}) async-start(), calls=%async_computation.4 | async-start | bytes 7077888 | tf_op jit(solution)/shard_map/all_gather | solution.py:168
  41.6 14.9 %collective-permute-start.5 = (bf16[256,512]{1,0:T(8,128)(2,1)S(1)}, bf16[256,512]{1,0:T(8,128)(2,1)S(1)}, u32[]{:S(2)}, u32[]{:S(2)}) collective-permute-start(bf16[256,512]{1,0:T(8,128)(2,1)S(1)} %constant_dynamic-slice_fusion.11), channel_id=1, source_target_pairs={{0,1},{1,2},{2,3},{3,0},{4,5},{5,6},{6,7},{7,4},{8,9},{9,10},{10,1... | collective-permute-start | bytes 786440 | tf_op jit(solution)/shard_map/ppermute | solution.py:130
  47.4 18.5 %collective-permute-start.4 = (bf16[256,512]{1,0:T(8,128)(2,1)S(1)}, bf16[256,512]{1,0:T(8,128)(2,1)S(1)}, u32[]{:S(2)}, u32[]{:S(2)}) collective-permute-start(bf16[256,512]{1,0:T(8,128)(2,1)S(1)} %constant_dynamic-slice_fusion.11), channel_id=1, source_target_pairs={{0,2},{1,3},{2,0},{3,1},{4,6},{5,7},{6,4},{7,5},{8,10},{9,11},{10,... | collective-permute-start | bytes 786440 | tf_op jit(solution)/shard_map/ppermute | solution.py:130
  49.6 16.2 %collective-permute-start.3 = (bf16[256,512]{1,0:T(8,128)(2,1)S(1)}, bf16[256,512]{1,0:T(8,128)(2,1)S(1)}, u32[]{:S(2)}, u32[]{:S(2)}) collective-permute-start(bf16[256,512]{1,0:T(8,128)(2,1)S(1)} %constant_dynamic-slice_fusion.11), channel_id=1, source_target_pairs={{0,3},{1,0},{2,1},{3,2},{4,7},{5,4},{6,5},{7,6},{8,11},{9,8},{10,9... | collective-permute-start | bytes 786440 | tf_op jit(solution)/shard_map/ppermute | solution.py:130
  66.8 123.2 %all-gather.11.cloned.1.call-start = ((), (), s32[]{:S(2)}) async-start(), calls=%async_computation.5 | async-start | bytes 7077888 | tf_op jit(solution)/shard_map/all_gather | solution.py:169
  68.6 14.8 %collective-permute-start.8 = (bf16[128,1024]{1,0:T(8,128)(2,1)}, bf16[128,1024]{1,0:T(8,128)(2,1)}, u32[]{:S(2)}, u32[]{:S(2)}) collective-permute-start(bf16[128,1024]{1,0:T(8,128)(2,1)} %constant_dynamic-slice_fusion.10), channel_id=1, source_target_pairs={{0,1},{1,2},{2,3},{3,0},{4,5},{5,6},{6,7},{7,4},{8,9},{9,10},{10,1... | collective-permute-start | bytes 786440 | tf_op jit(solution)/shard_map/ppermute | solution.py:130
  74.7 18.7 %collective-permute-start.7 = (bf16[128,1024]{1,0:T(8,128)(2,1)}, bf16[128,1024]{1,0:T(8,128)(2,1)}, u32[]{:S(2)}, u32[]{:S(2)}) collective-permute-start(bf16[128,1024]{1,0:T(8,128)(2,1)} %constant_dynamic-slice_fusion.10), channel_id=1, source_target_pairs={{0,2},{1,3},{2,0},{3,1},{4,6},{5,7},{6,4},{7,5},{8,10},{9,11},{10,... | collective-permute-start | bytes 786440 | tf_op jit(solution)/shard_map/ppermute | solution.py:130
  76.3 17.1 %collective-permute-start.6 = (bf16[128,1024]{1,0:T(8,128)(2,1)}, bf16[128,1024]{1,0:T(8,128)(2,1)}, u32[]{:S(2)}, u32[]{:S(2)}) collective-permute-start(bf16[128,1024]{1,0:T(8,128)(2,1)} %constant_dynamic-slice_fusion.10), channel_id=1, source_target_pairs={{0,3},{1,0},{2,1},{3,2},{4,7},{5,4},{6,5},{7,6},{8,11},{9,8},{10,9... | collective-permute-start | bytes 786440 | tf_op jit(solution)/shard_map/ppermute | solution.py:130
  95.5 280.1 %reduce-scatter.4.cloned.1.call-start = ((), (), s32[]{:S(2)}) async-start(), calls=%async_computation.6 | async-start | bytes 5242880 | tf_op jit(solution)/shard_map/reduce_scatter | solution.py:230
  114.8 9.4 %copy-start.8 = (bf16[512,1024]{0,1:T(8,128)(2,1)}, bf16[512,1024]{0,1:T(8,128)(2,1)S(1)}, u32[]{:S(2)}) copy-start(bf16[512,1024]{0,1:T(8,128)(2,1)S(1)} %copy.70) | copy-start | bytes 3145732
  190.0 9.1 %copy-start.11 = (bf16[1,512,1024]{2,1,0:T(8,128)(2,1)S(1)}, bf16[1,512,1024]{2,1,0:T(8,128)(2,1)}, u32[]{:S(2)}) copy-start(bf16[1,512,1024]{2,1,0:T(8,128)(2,1)} %param.19) | copy-start | bytes 3145732
  190.0 9.1 %copy-start.36 = (f32[1,2,4,128]{3,1,2,0:T(2,128)S(1)}, f32[1,2,4,128]{3,1,2,0:T(2,128)}, u32[]{:S(2)}) copy-start(f32[1,2,4,128]{3,1,2,0:T(2,128)} %copy.111) | copy-start | bytes 12292
  248.7 8.6 %copy-start.20 = (bf16[512,1024]{0,1:T(8,128)(2,1)S(1)}, bf16[512,1024]{0,1:T(8,128)(2,1)}, u32[]{:S(2)}) copy-start(bf16[512,1024]{0,1:T(8,128)(2,1)} %copy.68) | copy-start | bytes 3145732
  257.4 27.5 %copy-start.21 = (bf16[16,64,512]{2,1,0:T(8,128)(2,1)}, bf16[16,64,512]{2,1,0:T(8,128)(2,1)S(1)}, u32[]{:S(2)}) copy-start(bf16[16,64,512]{2,1,0:T(8,128)(2,1)S(1)} %get-tuple-element.75) | copy-start | bytes 3145732
  268.8 12.0 %copy-start.10 = (bf16[512,1024]{0,1:T(8,128)(2,1)S(1)}, bf16[512,1024]{0,1:T(8,128)(2,1)}, u32[]{:S(2)}) copy-start(bf16[512,1024]{0,1:T(8,128)(2,1)} %copy.69) | copy-start | bytes 3145732
  287.3 12.2 %collective-permute-start.10 = (bf16[512,1536]{0,1:T(8,128)(2,1)}, bf16[512,1536]{0,1:T(8,128)(2,1)}, u32[]{:S(2)}, u32[]{:S(2)}) collective-permute-start(bf16[512,1536]{0,1:T(8,128)(2,1)} %bitcast.26), channel_id=1, source_target_pairs={{0,4},{4,0},{1,5},{5,1},{2,6},{6,2},{3,7},{7,3},{8,12},{12,8},{9,1... | collective-permute-start | bytes 4718600 | tf_op jit(solution)/shard_map/ppermute | solution.py:136
  287.6 10.0 %collective-permute-start.11 = (bf16[512,1024]{0,1:T(8,128)(2,1)}, bf16[512,1024]{0,1:T(8,128)(2,1)}, u32[]{:S(2)}, u32[]{:S(2)}) collective-permute-start(bf16[512,1024]{0,1:T(8,128)(2,1)} %fusion.55), channel_id=1, source_target_pairs={{0,4},{4,0},{1,5},{5,1},{2,6},{6,2},{3,7},{7,3},{8,12},{12,8},{9,1... | collective-permute-start | bytes 3145736 | tf_op jit(solution)/shard_map/ppermute | solution.py:136
  287.8 11.7 %collective-permute-start.9 = (bf16[512,1024]{1,0:T(8,128)(2,1)}, bf16[512,1024]{1,0:T(8,128)(2,1)}, u32[]{:S(2)}, u32[]{:S(2)}) collective-permute-start(bf16[512,1024]{1,0:T(8,128)(2,1)} %fusion.56), channel_id=1, source_target_pairs={{0,4},{4,0},{1,5},{5,1},{2,6},{6,2},{3,7},{7,3},{8,12},{12,8},{9,1... | collective-permute-start | bytes 3145736 | tf_op jit(solution)/shard_map/ppermute | solution.py:136
  292.3 5.3 collective-permute-start.12
  305.9 110.0 %reduce-scatter.6.cloned.1.call-start = ((), (), s32[]{:S(2)}) async-start(), calls=%async_computation.8 | async-start | bytes 5242880 | tf_op jit(solution)/shard_map/reduce_scatter | solution.py:230
  334.4 15.5 %collective-permute-start.17 = (bf16[512,2048]{0,1:T(8,128)(2,1)S(1)}, bf16[512,2048]{0,1:T(8,128)(2,1)}, u32[]{:S(2)}, u32[]{:S(2)}) collective-permute-start(bf16[512,2048]{0,1:T(8,128)(2,1)S(1)} %bitcast.193), channel_id=1, source_target_pairs={{0,4},{4,0},{1,5},{5,1},{2,6},{6,2},{3,7},{7,3},{8,12},{12,8},{9,1... | collective-permute-start | bytes 6291464 | tf_op jit(solution)/shard_map/ppermute | solution.py:136
  334.7 15.1 %collective-permute-start.16 = (bf16[512,1024]{1,0:T(8,128)(2,1)}, bf16[512,1024]{1,0:T(8,128)(2,1)}, u32[]{:S(2)}, u32[]{:S(2)}) collective-permute-start(bf16[512,1024]{1,0:T(8,128)(2,1)} %copy-done.29), channel_id=1, source_target_pairs={{0,4},{4,0},{1,5},{5,1},{2,6},{6,2},{3,7},{7,3},{8,12},{12,8},{9,1... | collective-permute-start | bytes 3145736 | tf_op jit(solution)/shard_map/ppermute | solution.py:136
  356.1 115.9 %reduce-scatter.8.cloned.1.call-start = ((), (), s32[]{:S(2)}) async-start(), calls=%async_computation.10 | async-start | bytes 5242880 | tf_op jit(solution)/shard_map/reduce_scatter | solution.py:241
  365.3 5.7 collective-permute-start.21
  365.8 5.3 collective-permute-start.22
  375.6 178.2 %all-gather.13.cloned.1.call-start = ((), (), s32[]{:S(2)}) async-start(), calls=%async_computation.7 | async-start | bytes 2359296 | tf_op jit(solution)/shard_map/all_gather | solution.py:232
  376.9 10.6 %collective-permute-start.15 = (bf16[256,512]{1,0:T(8,128)(2,1)S(1)}, bf16[256,512]{1,0:T(8,128)(2,1)S(1)}, u32[]{:S(2)}, u32[]{:S(2)}) collective-permute-start(bf16[256,512]{1,0:T(8,128)(2,1)S(1)} %get-tuple-element.46), channel_id=1, source_target_pairs={{0,3},{1,0},{2,1},{3,2},{4,7},{5,4},{6,5},{7,6},{8,11},{9,8},{10,9... | collective-permute-start | bytes 786440 | tf_op jit(solution)/shard_map/ppermute | solution.py:133
  380.7 23.3 %collective-permute-start.14 = (bf16[256,512]{1,0:T(8,128)(2,1)S(1)}, bf16[256,512]{1,0:T(8,128)(2,1)S(1)}, u32[]{:S(2)}, u32[]{:S(2)}) collective-permute-start(bf16[256,512]{1,0:T(8,128)(2,1)S(1)} %get-tuple-element.47), channel_id=1, source_target_pairs={{0,2},{1,3},{2,0},{3,1},{4,6},{5,7},{6,4},{7,5},{8,10},{9,11},{10,... | collective-permute-start | bytes 786440 | tf_op jit(solution)/shard_map/ppermute | solution.py:133
  380.9 23.2 %collective-permute-start.13 = (bf16[256,512]{1,0:T(8,128)(2,1)S(1)}, bf16[256,512]{1,0:T(8,128)(2,1)S(1)}, u32[]{:S(2)}, u32[]{:S(2)}) collective-permute-start(bf16[256,512]{1,0:T(8,128)(2,1)S(1)} %get-tuple-element.45), channel_id=1, source_target_pairs={{0,1},{1,2},{2,3},{3,0},{4,5},{5,6},{6,7},{7,4},{8,9},{9,10},{10,1... | collective-permute-start | bytes 786440 | tf_op jit(solution)/shard_map/ppermute | solution.py:133
  405.9 137.6 %copy-start.14 = (bf16[16,64,512]{2,1,0:T(8,128)(2,1)S(1)}, bf16[16,64,512]{2,1,0:T(8,128)(2,1)}, u32[]{:S(2)}) copy-start(bf16[16,64,512]{2,1,0:T(8,128)(2,1)} %copy-done.13) | copy-start | bytes 3145732
  405.9 137.6 %copy-start.22 = (bf16[16,64,512]{2,1,0:T(8,128)(2,1)S(1)}, bf16[16,64,512]{2,1,0:T(8,128)(2,1)}, u32[]{:S(2)}) copy-start(bf16[16,64,512]{2,1,0:T(8,128)(2,1)} %copy-done.21) | copy-start | bytes 3145732
  405.9 152.5 %all-gather.15.cloned.1.call-start = ((), (), s32[]{:S(2)}) async-start(), calls=%async_computation.9 | async-start | bytes 2359296 | tf_op jit(solution)/shard_map/all_gather | solution.py:232
  417.0 10.1 %collective-permute-start.20 = (bf16[256,512]{1,0:T(8,128)(2,1)S(1)}, bf16[256,512]{1,0:T(8,128)(2,1)S(1)}, u32[]{:S(2)}, u32[]{:S(2)}) collective-permute-start(bf16[256,512]{1,0:T(8,128)(2,1)S(1)} %get-tuple-element.43), channel_id=1, source_target_pairs={{0,3},{1,0},{2,1},{3,2},{4,7},{5,4},{6,5},{7,6},{8,11},{9,8},{10,9... | collective-permute-start | bytes 786440 | tf_op jit(solution)/shard_map/ppermute | solution.py:133
  420.4 22.5 %collective-permute-start.19 = (bf16[256,512]{1,0:T(8,128)(2,1)S(1)}, bf16[256,512]{1,0:T(8,128)(2,1)S(1)}, u32[]{:S(2)}, u32[]{:S(2)}) collective-permute-start(bf16[256,512]{1,0:T(8,128)(2,1)S(1)} %get-tuple-element.44), channel_id=1, source_target_pairs={{0,2},{1,3},{2,0},{3,1},{4,6},{5,7},{6,4},{7,5},{8,10},{9,11},{10,... | collective-permute-start | bytes 786440 | tf_op jit(solution)/shard_map/ppermute | solution.py:133
  420.4 22.5 %collective-permute-start.18 = (bf16[256,512]{1,0:T(8,128)(2,1)S(1)}, bf16[256,512]{1,0:T(8,128)(2,1)S(1)}, u32[]{:S(2)}, u32[]{:S(2)}) collective-permute-start(bf16[256,512]{1,0:T(8,128)(2,1)S(1)} %get-tuple-element.42), channel_id=1, source_target_pairs={{0,1},{1,2},{2,3},{3,0},{4,5},{5,6},{6,7},{7,4},{8,9},{9,10},{10,1... | collective-permute-start | bytes 786440 | tf_op jit(solution)/shard_map/ppermute | solution.py:133
  444.7 119.7 %all-gather.17.cloned.1.call-start = ((), (), s32[]{:S(2)}) async-start(), calls=%async_computation.11 | async-start | bytes 2359296 | tf_op jit(solution)/shard_map/all_gather | solution.py:247
  473.2 10.1 %collective-permute-start.25 = (bf16[128,1024]{1,0:T(8,128)(2,1)S(1)}, bf16[128,1024]{1,0:T(8,128)(2,1)S(1)}, u32[]{:S(2)}, u32[]{:S(2)}) collective-permute-start(bf16[128,1024]{1,0:T(8,128)(2,1)S(1)} %get-tuple-element.40), channel_id=1, source_target_pairs={{0,3},{1,0},{2,1},{3,2},{4,7},{5,4},{6,5},{7,6},{8,11},{9,8},{10,9... | collective-permute-start | bytes 786440 | tf_op jit(solution)/shard_map/ppermute | solution.py:133
  476.5 22.5 %collective-permute-start.24 = (bf16[128,1024]{1,0:T(8,128)(2,1)S(1)}, bf16[128,1024]{1,0:T(8,128)(2,1)S(1)}, u32[]{:S(2)}, u32[]{:S(2)}) collective-permute-start(bf16[128,1024]{1,0:T(8,128)(2,1)S(1)} %get-tuple-element.41), channel_id=1, source_target_pairs={{0,2},{1,3},{2,0},{3,1},{4,6},{5,7},{6,4},{7,5},{8,10},{9,11},{10,... | collective-permute-start | bytes 786440 | tf_op jit(solution)/shard_map/ppermute | solution.py:133
  476.5 22.5 %collective-permute-start.23 = (bf16[128,1024]{1,0:T(8,128)(2,1)S(1)}, bf16[128,1024]{1,0:T(8,128)(2,1)S(1)}, u32[]{:S(2)}, u32[]{:S(2)}) collective-permute-start(bf16[128,1024]{1,0:T(8,128)(2,1)S(1)} %get-tuple-element.39), channel_id=1, source_target_pairs={{0,1},{1,2},{2,3},{3,0},{4,5},{5,6},{6,7},{7,4},{8,9},{9,10},{10,1... | collective-permute-start | bytes 786440 | tf_op jit(solution)/shard_map/ppermute | solution.py:133
  558.4 10.0 %copy-start.1 = (bf16[256,4096]{1,0:T(8,128)(2,1)S(1)}, bf16[256,4096]{1,0:T(8,128)(2,1)}, u32[]{:S(2)}) copy-start(bf16[256,4096]{1,0:T(8,128)(2,1)} %param.26) | copy-start | bytes 6291460
  (30 other events, 113.3 us)
Sparse Core Ops, SparseCore 0:
  41.6 51.7 all-gather.6
  95.9 46.6 all-gather.8
  144.5 45.5 all-gather.10
  306.0 54.0 reduce-scatter.3
  363.2 52.6 reduce-scatter.5
  419.3 52.6 reduce-scatter.7
  474.6 28.1 all-gather.12
  505.4 28.3 all-gather.14
  536.5 27.8 all-gather.16
where the time goes:
time: 581 us; the launch traced here: 575 us
  waiting for transfers between devices  157 us (27%)
  matrix products  147 us (25%)
  local copies, waits for them, and re-layouts  89.9 us (15%)
  other arithmetic  84.6 us (15%)
  starting transfers between devices  40.7 us (7%)
  blocking collectives  40.2 us (7%)
  between operations  15.8 us (3%)
    ppermute x9, waiting for transfers between devices, to_shard(): lax.ppermute(value, 'shard', [(i, (i + step) % group) for i in range(grou...  65.1 us
    dot_general x8, matrix products, matmul(): return jnp.dot(left, right, preferred_element_type=jnp.float32)  51.7 us
    ppermute x9, waiting for transfers between devices, from_shard(): lax.ppermute(value, 'shard', [(i, (i - step) % group) for i in range(grou...  46.6 us
    psum x1, blocking collectives, local(): small = lax.psum(small, ALL)  40.2 us
    unnamed x118, local copies, waits for them, and re-layouts  35 us
    dot_general x8, matrix products, outer_sum(): lax.dot_general(left, right, (((0,), (0,)), ((), ())), preferred_element_...  28.1 us
    reduce_scatter x1, waiting for transfers between devices, local(): lax.psum_scatter(grad_down.reshape(group, chips * part_down, model_width)...  27.2 us
    dot_general x8, matrix products, project_back(): lax.dot_general(left, right, (((1,), (1,)), ((), ())), preferred_element_...  25.8 us
  transfers between devices with their start and end apart: 35, of which 17 were waited for; matrix products, arithmetic and copies ran while one was open for 35% of the time, Pallas kernels for 0%

commit v1 on v0

--- a/solution.py
+++ b/solution.py
@@ -290,7 +290,8 @@
         grad_stwo,
     )
     small = jnp.concatenate([v.reshape(group, -1) for v in small], axis=1)
-    small = lax.psum(small, ALL)
+    terms = lax.all_gather(small, ALL, axis=0, tiled=False)
+    small = terms.sum(axis=0)
     small = lax.dynamic_index_in_dim(small, own, axis=0, keepdims=False)
     vecs, start = ([], 0)
     for size in sizes:

time: 581 us -> 644 us (1.11)
  waiting for transfers between devices: 157 us -> 258 us
  blocking collectives: 40.2 us -> 0 us
    all_gather x2, waiting for transfers between devices: 0.01 us -> 52.3 us  [scatter_columns(): return lax.all_gather(share, REP, axis=1, tiled=True).astype(jnp.float32)]
    psum x1 -> x0, blocking collectives: 40.2 us -> none  [local(): small = lax.psum(small, ALL)]
    all_gather x1, waiting for transfers between devices: 1.69 us -> 26.1 us  [local(): lax.all_gather(own_sum(grad_down), REP, axis=0, tiled=True)]
    all_gather x0 -> x1, waiting for transfers between devices: none -> 24.4 us  [local(): terms = lax.all_gather(small, ALL, axis=0, tiled=False)]
  transfers between devices with their start and end apart: 35 -> 36, of which waited for: 17 -> 20; matrix products, arithmetic and copies ran while one was open for 35% -> 32% of each run, Pallas kernels for 0% -> 0%
where the time goes in v1:
time: 644 us; the launch traced here: 638 us
  waiting for transfers between devices  258 us (40%)
  matrix products  147 us (23%)
  local copies, waits for them, and re-layouts  90.2 us (14%)
  other arithmetic  86.2 us (13%)
  starting transfers between devices  40.9 us (6%)
  between operations  16.2 us (3%)
    ppermute x9, waiting for transfers between devices, to_shard(): lax.ppermute(value, 'shard', [(i, (i + step) % group) for i in range(grou...  66.5 us
    all_gather x2, waiting for transfers between devices, scatter_columns(): return lax.all_gather(share, REP, axis=1, tiled=True).astype(jnp.float32)  52.3 us
    dot_general x8, matrix products, matmul(): return jnp.dot(left, right, preferred_element_type=jnp.float32)  51.8 us
    ppermute x9, waiting for transfers between devices, from_shard(): lax.ppermute(value, 'shard', [(i, (i - step) % group) for i in range(grou...  46.6 us
    unnamed x118, local copies, waits for them, and re-layouts  35.6 us
    dot_general x8, matrix products, outer_sum(): lax.dot_general(left, right, (((0,), (0,)), ((), ())), preferred_element_...  28.2 us
    reduce_scatter x1, waiting for transfers between devices, local(): lax.psum_scatter(grad_down.reshape(group, chips * part_down, model_width)...  27.2 us
    all_gather x1, waiting for transfers between devices, local(): lax.all_gather(own_sum(grad_down), REP, axis=0, tiled=True)  26.1 us
  transfers between devices with their start and end apart: 36, of which 20 were waited for; matrix products, arithmetic and copies ran while one was open for 32% of the time, Pallas kernels for 0%

profile of v1, /device:TPU:0, one launch (start us, length us, event | category | flops | bytes accessed | tf_op | source)
XLA Modules:
  0.0 638.5 jit_solution(5440367019682887224)
XLA Ops:
  22.3 5.7 collective-permute-done.2
  28.0 11.1 %collective-permute-done.1 = bf16[272,512]{1,0:T(8,128)(2,1)S(1)} collective-permute-done((bf16[272,512]{1,0:T(8,128)(2,1)S(1)}, bf16[272,512]{1,0:T(8,128)(2,1)S(1)}, u32[]{:S(2)}, u32[]{:S(2)}) %collective-permute-start.1) | collective-permute-done | bytes 278560 | tf_op jit(solution)/shard_map/ppermute | solution.py:130
  41.6 5.8 collective-permute-start.5
  49.8 6.6 %collective-permute-done.5 = bf16[256,512]{1,0:T(8,128)(2,1)S(1)} collective-permute-done((bf16[256,512]{1,0:T(8,128)(2,1)S(1)}, bf16[256,512]{1,0:T(8,128)(2,1)S(1)}, u32[]{:S(2)}, u32[]{:S(2)}) %collective-permute-start.5) | collective-permute-done | bytes 262176 | tf_op jit(solution)/shard_map/ppermute | solution.py:130
  56.4 9.4 %collective-permute-done.4 = bf16[256,512]{1,0:T(8,128)(2,1)S(1)} collective-permute-done((bf16[256,512]{1,0:T(8,128)(2,1)S(1)}, bf16[256,512]{1,0:T(8,128)(2,1)S(1)}, u32[]{:S(2)}, u32[]{:S(2)}) %collective-permute-start.4) | collective-permute-done | bytes 262176 | tf_op jit(solution)/shard_map/ppermute | solution.py:130
  68.6 6.1 collective-permute-start.8
  79.7 3.7 collective-permute-done.8
  83.4 10.0 %collective-permute-done.7 = bf16[128,1024]{1,0:T(8,128)(2,1)} collective-permute-done((bf16[128,1024]{1,0:T(8,128)(2,1)}, bf16[128,1024]{1,0:T(8,128)(2,1)}, u32[]{:S(2)}, u32[]{:S(2)}) %collective-permute-start.7) | collective-permute-done | bytes 262176 | tf_op jit(solution)/shard_map/ppermute | solution.py:130
  100.2 4.8 fusion.18
  114.8 9.4 %fusion.82 = (f32[16,512]{1,0:T(8,128)S(1)}, f32[16,512,512]{1,2,0:T(8,128)}) fusion(bf16[512,16,64]{0,2,1:T(8,128)(2,1)} %bitcast.175, bf16[512,16,64]{0,2,1:T(8,128)(2,1)S(1)} %bitcast.173, pred[512,512]{0,1:T(8,128)(4,1)S(1)} %compare_and_fusion), kind=kOutput, calls=%fused_computation.211 | convolution fusion | flops 549445632 | bytes 19169280 | tf_op jit(solution)/shard_map/qhd,khd->hqk/dot_general | solution.py:49
  124.3 8.4 %fusion = f32[16,512]{1,0:T(8,128)S(1)} fusion(f32[16,512,512]{1,2,0:T(8,128)} %get-tuple-element.65, f32[16,512]{1,0:T(8,128)S(1)} %get-tuple-element.64), kind=kLoop, calls=%fused_computation.10 | loop fusion | flops 8380416 | bytes 16842752 | tf_op jit(solution)/shard_map/reduce_sum | solution.py:55
  132.6 7.7 %fusion.42 = bf16[16,64,512]{2,1,0:T(8,128)(2,1)S(1)} fusion(bf16[512,16,64]{0,2,1:T(8,128)(2,1)S(1)} %bitcast.185, f32[16,512,512]{1,2,0:T(8,128)} %get-tuple-element.65, f32[16,512]{1,0:T(8,128)S(1)} %fusion, f32[16,512]{1,0:T(8,128)S(1)} %get-tuple-element.64), kind=kOutput, calls=%fused_computation.115 | convolution fusion | flops 549978112 | bytes 18939904 | tf_op jit(solution)/shard_map/hqk,khd->qhd/dot_general | solution.py:57
  149.9 4.6 fusion.67
  154.5 24.8 %multiply_convert_fusion.1 = (bf16[512,4096]{1,0:T(8,128)(2,1)S(1)}, f32[512,4096]{1,0:T(8,128)}) fusion(f32[4096]{0:T(1024)S(1)} %bitcast.220, f32[512,4096]{1,0:T(8,128)} %fusion.67, bf16[768,4096]{1,0:T(8,128)(2,1)} %all-gather.12.cloned.1.call-done, bf16[512,1024]{1,0:T(8,128)(2,1)S(1)} %fusion.54), kind=kOutput, calls=%fused_computation.25 | convolution fusion | flops 3361734656 | bytes 28065792 | tf_op jit(solution)/shard_map/dot_general | solution.py:21
  186.4 3.7 all-gather.14.cloned.1.call-done
  190.1 8.7 %fusion.84 = (f32[512]{0:T(512)S(1)}, f32[512,1024]{1,0:T(8,128)S(1)}) fusion(f32[1024]{0:T(1024)S(1)} %bitcast.222, f32[512,1024]{1,0:T(8,128)} %fusion.57, bf16[3072,1024]{1,0:T(8,128)(2,1)} %bitcast.231, bf16[512,4096]{1,0:T(8,128)(2,1)} %copy-done.6, f32[1024]{0:T(1024)S(1)} %bitcast.216, f32[1024]{0:T(1024)S(1)} %bitcast.209, f32[512]{0:T(512)S(1)} %fusion.72, ...), kind=kOutput, calls=%fused_computation.213 | convolution fusion | flops 3225419264 | bytes 15747072 | tf_op jit(solution)/shard_map/dot_general | solution.py:21
  202.2 6.1 fusion.86
  209.7 23.1 %convert_reduce_fusion = (f32[4096]{0:T(1024)S(1)}, bf16[512,4096]{1,0:T(8,128)(2,1)S(1)}) fusion(f32[512,4096]{1,0:T(8,128)S(1)} %bitcast.180, s32[]{:T(128)S(6)} %select_n.73, f32[512,3072]{1,0:T(8,128)S(1)} %fusion.86, f32[512,1024]{1,0:T(8,128)S(1)} %fusion.85), kind=kLoop, calls=%fused_computation.22 | loop fusion | flops 161476608 | bytes 20987908 | tf_op jit(solution)/shard_map/reduce_sum | solution.py:37
  234.3 5.9 fusion.88
  248.7 8.6 %convert_reduce_fusion.4 = (f32[16,64]{1,0:T(8,128)S(1)}, bf16[16,64,512]{2,1,0:T(8,128)(2,1)S(1)}) fusion(bf16[512,16,64]{0,2,1:T(8,128)(2,1)S(1)} %bitcast.177, f32[16,512,512]{1,2,0:T(8,128)} %get-tuple-element.65, f32[16,512]{1,0:T(8,128)S(1)} %log_add_fusion), kind=kOutput, calls=%fused_computation.100 | convolution fusion | flops 546831360 | bytes 18911232 | tf_op jit(solution)/shard_map/hqk,qhd->khd/dot_general | solution.py:85
  257.4 11.4 %multiply_reduce_fusion = (f32[16,512]{1,0:T(8,128)S(1)}, f32[16,512,512]{1,2,0:T(8,128)}) fusion(f32[16,512,512]{1,2,0:T(8,128)} %get-tuple-element.65, f32[16,512]{1,0:T(8,128)S(1)} %log_add_fusion, bf16[512,16,64]{0,2,1:T(8,128)(2,1)S(1)} %bitcast.178, bf16[512,16,64]{0,2,1:T(8,128)(2,1)S(1)} %bitcast.186), kind=kOutput, calls=%fused_computation.5 | convolution fusion | flops 549445632 | bytes 35717120 | tf_op jit(solution)/shard_map/qhd,khd->hqk/dot_general | solution.py:71
  268.8 12.0 %multiply_convert_fusion = bf16[16,512,512]{1,2,0:T(8,128)(2,1)S(1)} fusion(f32[16,512,512]{1,2,0:T(8,128)} %get-tuple-element.73, f32[16,512,512]{1,2,0:T(8,128)} %get-tuple-element.65, f32[16,512]{1,0:T(8,128)S(1)} %get-tuple-element.72, f32[16,512]{1,0:T(8,128)S(1)} %log_add_fusion), kind=kLoop, calls=%fused_computation.4 | loop fusion | flops 16777216 | bytes 42008576 | tf_op jit(solution)/shard_map/convert_element_type | solution.py:77
  299.6 3.6 add_convert_fusion.3
  306.0 8.1 %reshape.403 = bf16[512,4,2,512]{3,2,1,0:T(2,128)(2,1)} reshape(bf16[512,4096]{1,0:T(8,128)(2,1)} %copy-done.7) | data formatting | bytes 8388608 | tf_op jit(solution)/shard_map/reshape | solution.py:209
  314.0 11.2 %constant_dynamic-slice_fusion.3 = (bf16[512,4,1,512]{3,2,1,0:T(2,128)(2,1)}, bf16[512,4,1,512]{3,2,1,0:T(2,128)(2,1)}) fusion(bf16[512,4,2,512]{3,2,1,0:T(2,128)(2,1)} %reshape.403, s32[]{:T(128)S(6)} %select_n.76, s32[]{:T(128)S(6)} %select_n.75), kind=kLoop, calls=%fused_computation.175 | loop fusion | bytes 8388616 | tf_op jit(solution)/shard_map/jit(dynamic_index_in_dim)/dynamic_slice | solution.py:210
  325.2 9.0 %copy.121 = bf16[512,4,1,512]{0,3,1,2:T(8,128)(2,1)S(1)} copy(bf16[512,4,1,512]{3,2,1,0:T(2,128)(2,1)} %get-tuple-element.34) | data formatting | bytes 4194304
  334.8 10.5 %copy.120 = bf16[512,4,1,512]{0,3,1,2:T(8,128)(2,1)} copy(bf16[512,4,1,512]{3,2,1,0:T(2,128)(2,1)} %get-tuple-element.35) | data formatting | bytes 4194304
  345.3 4.4 fusion.90
  349.8 6.3 add_convert_fusion.1
  356.1 6.5 %copy.109 = bf16[512,4096]{0,1:T(8,128)(2,1)} copy(bf16[512,4096]{1,0:T(8,128)(2,1)} %copy-done.6) | data formatting | bytes 8388608 | tf_op jit(solution)/shard_map/dynamic_slice | solution.py:140
  371.0 4.5 add_convert_fusion
  378.2 3.9 collective-permute-start.15
  383.0 5.9 collective-permute-done.15
  388.9 16.8 %collective-permute-done.14 = bf16[256,512]{1,0:T(8,128)(2,1)S(1)} collective-permute-done((bf16[256,512]{1,0:T(8,128)(2,1)S(1)}, bf16[256,512]{1,0:T(8,128)(2,1)S(1)}, u32[]{:S(2)}, u32[]{:S(2)}) %collective-permute-start.14) | collective-permute-done | bytes 262176 | tf_op jit(solution)/shard_map/ppermute | solution.py:133
  407.5 8.4 %reduce-scatter.6.cloned.1.call-done = bf16[1024,512]{1,0:T(8,128)(2,1)} async-done(((bf16[1024,2048]{1,0:T(8,128)(2,1)}), bf16[1024,512]{1,0:T(8,128)(2,1)}) %reduce-scatter.6.cloned.1.call-update) | async-done | bytes 1048592 | tf_op jit(solution)/shard_map/reduce_scatter | solution.py:230
  421.6 5.7 collective-permute-done.20
  427.3 15.7 %collective-permute-done.19 = bf16[256,512]{1,0:T(8,128)(2,1)S(1)} collective-permute-done((bf16[256,512]{1,0:T(8,128)(2,1)S(1)}, bf16[256,512]{1,0:T(8,128)(2,1)S(1)}, u32[]{:S(2)}, u32[]{:S(2)}) %collective-permute-start.19) | collective-permute-done | bytes 262176 | tf_op jit(solution)/shard_map/ppermute | solution.py:133
  444.9 27.2 %reduce-scatter.8.cloned.1.call-done = bf16[4,128,1024]{2,1,0:T(8,128)(2,1)} async-done(((bf16[4,512,1024]{2,1,0:T(8,128)(2,1)}), bf16[4,128,1024]{2,1,0:T(8,128)(2,1)}) %reduce-scatter.8.cloned.1.call-update) | async-done | bytes 1048592 | tf_op jit(solution)/shard_map/reduce_scatter | solution.py:241
  477.7 5.7 collective-permute-done.25
  483.4 16.8 %collective-permute-done.24 = bf16[128,1024]{1,0:T(8,128)(2,1)S(1)} collective-permute-done((bf16[128,1024]{1,0:T(8,128)(2,1)S(1)}, bf16[128,1024]{1,0:T(8,128)(2,1)S(1)}, u32[]{:S(2)}, u32[]{:S(2)}) %collective-permute-start.24) | collective-permute-done | bytes 262176 | tf_op jit(solution)/shard_map/ppermute | solution.py:133
  504.8 5.2 fusion.16
  511.9 24.4 %all-gather.22.cloned.1.call-done = f32[32,4,3072]{2,1,0:T(4,128)} async-done(((f32[1,4,3072]{2,1,0:T(4,128)}), f32[32,4,3072]{2,1,0:T(4,128)}) %all-gather.22.cloned.1.call-update) | async-done | bytes 1572880 | tf_op jit(solution)/shard_map/all_gather | solution.py:293
  539.9 26.2 %all-gather.16.cloned.1.call-done = bf16[256,4096]{1,0:T(8,128)(2,1)} async-done(((bf16[256,512]{1,0:T(8,128)(2,1)}), bf16[256,4096]{1,0:T(8,128)(2,1)}) %all-gather.16.cloned.1.call-update) | async-done | bytes 2097168 | tf_op jit(solution)/shard_map/all_gather | solution.py:232
  566.1 3.6 slice.278
  570.7 26.2 %all-gather.18.cloned.1.call-done = bf16[256,4096]{1,0:T(8,128)(2,1)} async-done(((bf16[256,512]{1,0:T(8,128)(2,1)}), bf16[256,4096]{1,0:T(8,128)(2,1)}) %all-gather.18.cloned.1.call-update) | async-done | bytes 2097168 | tf_op jit(solution)/shard_map/all_gather | solution.py:232
  596.9 4.2 convert_element_type.279
  601.1 26.1 %all-gather.20.cloned.1.call-done = bf16[1024,1024]{1,0:T(8,128)(2,1)} async-done(((bf16[128,1024]{1,0:T(8,128)(2,1)}), bf16[1024,1024]{1,0:T(8,128)(2,1)}) %all-gather.20.cloned.1.call-update) | async-done | bytes 2097168 | tf_op jit(solution)/shard_map/all_gather | solution.py:247
  627.3 4.1 convert_element_type.287
  (273 shorter events, 134.6 us)
Async XLA Ops:
  7.2 34.3 %copy-start = (bf16[256,4096]{1,0:T(8,128)(2,1)S(1)}, bf16[256,4096]{1,0:T(8,128)(2,1)}, u32[]{:S(2)}) copy-start(bf16[256,4096]{1,0:T(8,128)(2,1)} %param.26) | copy-start | bytes 6291460
  7.2 93.0 %all-gather.10.cloned.1.call-start = ((), (), s32[]{:S(2)}) async-start(), calls=%async_computation.3 | async-start | bytes 7077888 | tf_op jit(solution)/shard_map/all_gather | solution.py:165
  15.2 62.5 %copy-start.17 = (bf16[1,512,1024]{2,1,0:T(8,128)(2,1)S(1)}, bf16[1,512,1024]{2,1,0:T(8,128)(2,1)}, u32[]{:S(2)}) copy-start(bf16[1,512,1024]{2,1,0:T(8,128)(2,1)} %param.16) | copy-start | bytes 3145732
  15.2 12.7 %collective-permute-start.2 = (bf16[272,512]{1,0:T(8,128)(2,1)S(1)}, bf16[272,512]{1,0:T(8,128)(2,1)S(1)}, u32[]{:S(2)}, u32[]{:S(2)}) collective-permute-start(bf16[272,512]{1,0:T(8,128)(2,1)S(1)} %pad_maximum_fusion.8), channel_id=1, source_target_pairs={{0,1},{1,2},{2,3},{3,0},{4,5},{5,6},{6,7},{7,4},{8,9},{9,10},{10,1... | collective-permute-start | bytes 835592 | tf_op jit(solution)/shard_map/ppermute | solution.py:130
  18.3 20.8 %collective-permute-start.1 = (bf16[272,512]{1,0:T(8,128)(2,1)S(1)}, bf16[272,512]{1,0:T(8,128)(2,1)S(1)}, u32[]{:S(2)}, u32[]{:S(2)}) collective-permute-start(bf16[272,512]{1,0:T(8,128)(2,1)S(1)} %pad_maximum_fusion.8), channel_id=1, source_target_pairs={{0,2},{1,3},{2,0},{3,1},{4,6},{5,7},{6,4},{7,5},{8,10},{9,11},{10,... | collective-permute-start | bytes 835592 | tf_op jit(solution)/shard_map/ppermute | solution.py:130
  20.9 18.2 %collective-permute-start = (bf16[272,512]{1,0:T(8,128)(2,1)S(1)}, bf16[272,512]{1,0:T(8,128)(2,1)S(1)}, u32[]{:S(2)}, u32[]{:S(2)}) collective-permute-start(bf16[272,512]{1,0:T(8,128)(2,1)S(1)} %pad_maximum_fusion.8), channel_id=1, source_target_pairs={{0,3},{1,0},{2,1},{3,2},{4,7},{5,4},{6,5},{7,6},{8,11},{9,8},{10,9... | collective-permute-start | bytes 835592 | tf_op jit(solution)/shard_map/ppermute | solution.py:130
  28.0 11.1 %copy-start.32 = (bf16[272,512]{1,0:T(8,128)(2,1)}, bf16[272,512]{1,0:T(8,128)(2,1)S(1)}, u32[]{:S(2)}) copy-start(bf16[272,512]{1,0:T(8,128)(2,1)S(1)} %collective-permute-done.2) | copy-start | bytes 835588
  39.1 40.3 %copy-start.40 = (s32[1,512]{1,0:T(1,128)S(1)}, s32[1,512]{1,0:T(1,128)}, u32[]{:S(2)}) copy-start(s32[1,512]{1,0:T(1,128)} %param.17) | copy-start | bytes 6148
  41.5 113.0 %all-gather.12.cloned.1.call-start = ((), (), s32[]{:S(2)}) async-start(), calls=%async_computation.4 | async-start | bytes 7077888 | tf_op jit(solution)/shard_map/all_gather | solution.py:168
  41.6 14.9 %collective-permute-start.5 = (bf16[256,512]{1,0:T(8,128)(2,1)S(1)}, bf16[256,512]{1,0:T(8,128)(2,1)S(1)}, u32[]{:S(2)}, u32[]{:S(2)}) collective-permute-start(bf16[256,512]{1,0:T(8,128)(2,1)S(1)} %constant_dynamic-slice_fusion.11), channel_id=1, source_target_pairs={{0,1},{1,2},{2,3},{3,0},{4,5},{5,6},{6,7},{7,4},{8,9},{9,10},{10,1... | collective-permute-start | bytes 786440 | tf_op jit(solution)/shard_map/ppermute | solution.py:130
  47.4 18.5 %collective-permute-start.4 = (bf16[256,512]{1,0:T(8,128)(2,1)S(1)}, bf16[256,512]{1,0:T(8,128)(2,1)S(1)}, u32[]{:S(2)}, u32[]{:S(2)}) collective-permute-start(bf16[256,512]{1,0:T(8,128)(2,1)S(1)} %constant_dynamic-slice_fusion.11), channel_id=1, source_target_pairs={{0,2},{1,3},{2,0},{3,1},{4,6},{5,7},{6,4},{7,5},{8,10},{9,11},{10,... | collective-permute-start | bytes 786440 | tf_op jit(solution)/shard_map/ppermute | solution.py:130
  49.6 16.2 %collective-permute-start.3 = (bf16[256,512]{1,0:T(8,128)(2,1)S(1)}, bf16[256,512]{1,0:T(8,128)(2,1)S(1)}, u32[]{:S(2)}, u32[]{:S(2)}) collective-permute-start(bf16[256,512]{1,0:T(8,128)(2,1)S(1)} %constant_dynamic-slice_fusion.11), channel_id=1, source_target_pairs={{0,3},{1,0},{2,1},{3,2},{4,7},{5,4},{6,5},{7,6},{8,11},{9,8},{10,9... | collective-permute-start | bytes 786440 | tf_op jit(solution)/shard_map/ppermute | solution.py:130
  66.8 123.2 %all-gather.14.cloned.1.call-start = ((), (), s32[]{:S(2)}) async-start(), calls=%async_computation.5 | async-start | bytes 7077888 | tf_op jit(solution)/shard_map/all_gather | solution.py:169
  68.6 14.8 %collective-permute-start.8 = (bf16[128,1024]{1,0:T(8,128)(2,1)}, bf16[128,1024]{1,0:T(8,128)(2,1)}, u32[]{:S(2)}, u32[]{:S(2)}) collective-permute-start(bf16[128,1024]{1,0:T(8,128)(2,1)} %constant_dynamic-slice_fusion.10), channel_id=1, source_target_pairs={{0,1},{1,2},{2,3},{3,0},{4,5},{5,6},{6,7},{7,4},{8,9},{9,10},{10,1... | collective-permute-start | bytes 786440 | tf_op jit(solution)/shard_map/ppermute | solution.py:130
  74.7 18.7 %collective-permute-start.7 = (bf16[128,1024]{1,0:T(8,128)(2,1)}, bf16[128,1024]{1,0:T(8,128)(2,1)}, u32[]{:S(2)}, u32[]{:S(2)}) collective-permute-start(bf16[128,1024]{1,0:T(8,128)(2,1)} %constant_dynamic-slice_fusion.10), channel_id=1, source_target_pairs={{0,2},{1,3},{2,0},{3,1},{4,6},{5,7},{6,4},{7,5},{8,10},{9,11},{10,... | collective-permute-start | bytes 786440 | tf_op jit(solution)/shard_map/ppermute | solution.py:130
  76.3 17.1 %collective-permute-start.6 = (bf16[128,1024]{1,0:T(8,128)(2,1)}, bf16[128,1024]{1,0:T(8,128)(2,1)}, u32[]{:S(2)}, u32[]{:S(2)}) collective-permute-start(bf16[128,1024]{1,0:T(8,128)(2,1)} %constant_dynamic-slice_fusion.10), channel_id=1, source_target_pairs={{0,3},{1,0},{2,1},{3,2},{4,7},{5,4},{6,5},{7,6},{8,11},{9,8},{10,9... | collective-permute-start | bytes 786440 | tf_op jit(solution)/shard_map/ppermute | solution.py:130
  95.5 281.5 %reduce-scatter.4.cloned.1.call-start = ((), (), s32[]{:S(2)}) async-start(), calls=%async_computation.6 | async-start | bytes 5242880 | tf_op jit(solution)/shard_map/reduce_scatter | solution.py:230
  114.8 9.4 %copy-start.8 = (bf16[512,1024]{0,1:T(8,128)(2,1)}, bf16[512,1024]{0,1:T(8,128)(2,1)S(1)}, u32[]{:S(2)}) copy-start(bf16[512,1024]{0,1:T(8,128)(2,1)S(1)} %copy.91) | copy-start | bytes 3145732
  190.0 9.1 %copy-start.11 = (bf16[1,512,1024]{2,1,0:T(8,128)(2,1)S(1)}, bf16[1,512,1024]{2,1,0:T(8,128)(2,1)}, u32[]{:S(2)}) copy-start(bf16[1,512,1024]{2,1,0:T(8,128)(2,1)} %param.19) | copy-start | bytes 3145732
  190.1 9.1 %copy-start.36 = (f32[1,2,4,128]{3,1,2,0:T(2,128)S(1)}, f32[1,2,4,128]{3,1,2,0:T(2,128)}, u32[]{:S(2)}) copy-start(f32[1,2,4,128]{3,1,2,0:T(2,128)} %copy.132) | copy-start | bytes 12292
  257.4 27.5 %copy-start.21 = (bf16[16,64,512]{2,1,0:T(8,128)(2,1)}, bf16[16,64,512]{2,1,0:T(8,128)(2,1)S(1)}, u32[]{:S(2)}) copy-start(bf16[16,64,512]{2,1,0:T(8,128)(2,1)S(1)} %get-tuple-element.75) | copy-start | bytes 3145732
  268.8 12.0 %copy-start.10 = (bf16[512,1024]{0,1:T(8,128)(2,1)S(1)}, bf16[512,1024]{0,1:T(8,128)(2,1)}, u32[]{:S(2)}) copy-start(bf16[512,1024]{0,1:T(8,128)(2,1)} %copy.90) | copy-start | bytes 3145732
  287.3 12.2 %collective-permute-start.10 = (bf16[512,1536]{0,1:T(8,128)(2,1)}, bf16[512,1536]{0,1:T(8,128)(2,1)}, u32[]{:S(2)}, u32[]{:S(2)}) collective-permute-start(bf16[512,1536]{0,1:T(8,128)(2,1)} %bitcast.26), channel_id=1, source_target_pairs={{0,4},{4,0},{1,5},{5,1},{2,6},{6,2},{3,7},{7,3},{8,12},{12,8},{9,1... | collective-permute-start | bytes 4718600 | tf_op jit(solution)/shard_map/ppermute | solution.py:136
  287.6 10.0 %collective-permute-start.11 = (bf16[512,1024]{0,1:T(8,128)(2,1)}, bf16[512,1024]{0,1:T(8,128)(2,1)}, u32[]{:S(2)}, u32[]{:S(2)}) collective-permute-start(bf16[512,1024]{0,1:T(8,128)(2,1)} %fusion.55), channel_id=1, source_target_pairs={{0,4},{4,0},{1,5},{5,1},{2,6},{6,2},{3,7},{7,3},{8,12},{12,8},{9,1... | collective-permute-start | bytes 3145736 | tf_op jit(solution)/shard_map/ppermute | solution.py:136
  287.9 11.7 %collective-permute-start.9 = (bf16[512,1024]{1,0:T(8,128)(2,1)}, bf16[512,1024]{1,0:T(8,128)(2,1)}, u32[]{:S(2)}, u32[]{:S(2)}) collective-permute-start(bf16[512,1024]{1,0:T(8,128)(2,1)} %fusion.56), channel_id=1, source_target_pairs={{0,4},{4,0},{1,5},{5,1},{2,6},{6,2},{3,7},{7,3},{8,12},{12,8},{9,1... | collective-permute-start | bytes 3145736 | tf_op jit(solution)/shard_map/ppermute | solution.py:136
  292.3 5.4 collective-permute-start.12
  305.9 110.0 %reduce-scatter.6.cloned.1.call-start = ((), (), s32[]{:S(2)}) async-start(), calls=%async_computation.8 | async-start | bytes 5242880 | tf_op jit(solution)/shard_map/reduce_scatter | solution.py:230
  334.2 15.5 %collective-permute-start.17 = (bf16[512,2048]{0,1:T(8,128)(2,1)S(1)}, bf16[512,2048]{0,1:T(8,128)(2,1)}, u32[]{:S(2)}, u32[]{:S(2)}) collective-permute-start(bf16[512,2048]{0,1:T(8,128)(2,1)S(1)} %bitcast.194), channel_id=1, source_target_pairs={{0,4},{4,0},{1,5},{5,1},{2,6},{6,2},{3,7},{7,3},{8,12},{12,8},{9,1... | collective-permute-start | bytes 6291464 | tf_op jit(solution)/shard_map/ppermute | solution.py:136
  334.6 15.1 %collective-permute-start.16 = (bf16[512,1024]{1,0:T(8,128)(2,1)}, bf16[512,1024]{1,0:T(8,128)(2,1)}, u32[]{:S(2)}, u32[]{:S(2)}) collective-permute-start(bf16[512,1024]{1,0:T(8,128)(2,1)} %copy-done.28), channel_id=1, source_target_pairs={{0,4},{4,0},{1,5},{5,1},{2,6},{6,2},{3,7},{7,3},{8,12},{12,8},{9,1... | collective-permute-start | bytes 3145736 | tf_op jit(solution)/shard_map/ppermute | solution.py:136
  356.1 116.0 %reduce-scatter.8.cloned.1.call-start = ((), (), s32[]{:S(2)}) async-start(), calls=%async_computation.10 | async-start | bytes 5242880 | tf_op jit(solution)/shard_map/reduce_scatter | solution.py:241
  365.3 5.7 collective-permute-start.21
  365.7 5.3 collective-permute-start.22
  375.5 160.8 %all-gather.22.cloned.1.call-start = ((), (), s32[]{:S(2)}) async-start(), calls=%async_computation.12 | async-start | bytes 1622016 | tf_op jit(solution)/shard_map/all_gather | solution.py:293
  376.7 189.3 %all-gather.16.cloned.1.call-start = ((), (), s32[]{:S(2)}) async-start(), calls=%async_computation.7 | async-start | bytes 2359296 | tf_op jit(solution)/shard_map/all_gather | solution.py:232
  378.2 123.8 %copy-start.14 = (bf16[16,64,512]{2,1,0:T(8,128)(2,1)S(1)}, bf16[16,64,512]{2,1,0:T(8,128)(2,1)}, u32[]{:S(2)}) copy-start(bf16[16,64,512]{2,1,0:T(8,128)(2,1)} %copy-done.13) | copy-start | bytes 3145732
  378.2 123.8 %copy-start.16 = (bf16[256,3072]{1,0:T(8,128)(2,1)S(1)}, bf16[256,3072]{1,0:T(8,128)(2,1)}, u32[]{:S(2)}) copy-start(bf16[256,3072]{1,0:T(8,128)(2,1)} %param.20) | copy-start | bytes 4718596
  378.2 10.6 %collective-permute-start.15 = (bf16[256,512]{1,0:T(8,128)(2,1)S(1)}, bf16[256,512]{1,0:T(8,128)(2,1)S(1)}, u32[]{:S(2)}, u32[]{:S(2)}) collective-permute-start(bf16[256,512]{1,0:T(8,128)(2,1)S(1)} %get-tuple-element.46), channel_id=1, source_target_pairs={{0,3},{1,0},{2,1},{3,2},{4,7},{5,4},{6,5},{7,6},{8,11},{9,8},{10,9... | collective-permute-start | bytes 786440 | tf_op jit(solution)/shard_map/ppermute | solution.py:133
  382.1 23.6 %collective-permute-start.14 = (bf16[256,512]{1,0:T(8,128)(2,1)S(1)}, bf16[256,512]{1,0:T(8,128)(2,1)S(1)}, u32[]{:S(2)}, u32[]{:S(2)}) collective-permute-start(bf16[256,512]{1,0:T(8,128)(2,1)S(1)} %get-tuple-element.47), channel_id=1, source_target_pairs={{0,2},{1,3},{2,0},{3,1},{4,6},{5,7},{6,4},{7,5},{8,10},{9,11},{10,... | collective-permute-start | bytes 786440 | tf_op jit(solution)/shard_map/ppermute | solution.py:133
  382.4 23.2 %collective-permute-start.13 = (bf16[256,512]{1,0:T(8,128)(2,1)S(1)}, bf16[256,512]{1,0:T(8,128)(2,1)S(1)}, u32[]{:S(2)}, u32[]{:S(2)}) collective-permute-start(bf16[256,512]{1,0:T(8,128)(2,1)S(1)} %get-tuple-element.45), channel_id=1, source_target_pairs={{0,1},{1,2},{2,3},{3,0},{4,5},{5,6},{6,7},{7,4},{8,9},{9,10},{10,1... | collective-permute-start | bytes 786440 | tf_op jit(solution)/shard_map/ppermute | solution.py:133
  407.5 189.4 %all-gather.18.cloned.1.call-start = ((), (), s32[]{:S(2)}) async-start(), calls=%async_computation.9 | async-start | bytes 2359296 | tf_op jit(solution)/shard_map/all_gather | solution.py:232
  417.1 10.1 %collective-permute-start.20 = (bf16[256,512]{1,0:T(8,128)(2,1)S(1)}, bf16[256,512]{1,0:T(8,128)(2,1)S(1)}, u32[]{:S(2)}, u32[]{:S(2)}) collective-permute-start(bf16[256,512]{1,0:T(8,128)(2,1)S(1)} %get-tuple-element.43), channel_id=1, source_target_pairs={{0,3},{1,0},{2,1},{3,2},{4,7},{5,4},{6,5},{7,6},{8,11},{9,8},{10,9... | collective-permute-start | bytes 786440 | tf_op jit(solution)/shard_map/ppermute | solution.py:133
  420.5 22.5 %collective-permute-start.19 = (bf16[256,512]{1,0:T(8,128)(2,1)S(1)}, bf16[256,512]{1,0:T(8,128)(2,1)S(1)}, u32[]{:S(2)}, u32[]{:S(2)}) collective-permute-start(bf16[256,512]{1,0:T(8,128)(2,1)S(1)} %get-tuple-element.44), channel_id=1, source_target_pairs={{0,2},{1,3},{2,0},{3,1},{4,6},{5,7},{6,4},{7,5},{8,10},{9,11},{10,... | collective-permute-start | bytes 786440 | tf_op jit(solution)/shard_map/ppermute | solution.py:133
  420.5 22.5 %collective-permute-start.18 = (bf16[256,512]{1,0:T(8,128)(2,1)S(1)}, bf16[256,512]{1,0:T(8,128)(2,1)S(1)}, u32[]{:S(2)}, u32[]{:S(2)}) collective-permute-start(bf16[256,512]{1,0:T(8,128)(2,1)S(1)} %get-tuple-element.42), channel_id=1, source_target_pairs={{0,1},{1,2},{2,3},{3,0},{4,5},{5,6},{6,7},{7,4},{8,9},{9,10},{10,1... | collective-permute-start | bytes 786440 | tf_op jit(solution)/shard_map/ppermute | solution.py:133
  444.8 182.5 %all-gather.20.cloned.1.call-start = ((), (), s32[]{:S(2)}) async-start(), calls=%async_computation.11 | async-start | bytes 2359296 | tf_op jit(solution)/shard_map/all_gather | solution.py:247
  473.3 10.1 %collective-permute-start.25 = (bf16[128,1024]{1,0:T(8,128)(2,1)S(1)}, bf16[128,1024]{1,0:T(8,128)(2,1)S(1)}, u32[]{:S(2)}, u32[]{:S(2)}) collective-permute-start(bf16[128,1024]{1,0:T(8,128)(2,1)S(1)} %get-tuple-element.40), channel_id=1, source_target_pairs={{0,3},{1,0},{2,1},{3,2},{4,7},{5,4},{6,5},{7,6},{8,11},{9,8},{10,9... | collective-permute-start | bytes 786440 | tf_op jit(solution)/shard_map/ppermute | solution.py:133
  476.6 23.5 %collective-permute-start.24 = (bf16[128,1024]{1,0:T(8,128)(2,1)S(1)}, bf16[128,1024]{1,0:T(8,128)(2,1)S(1)}, u32[]{:S(2)}, u32[]{:S(2)}) collective-permute-start(bf16[128,1024]{1,0:T(8,128)(2,1)S(1)} %get-tuple-element.41), channel_id=1, source_target_pairs={{0,2},{1,3},{2,0},{3,1},{4,6},{5,7},{6,4},{7,5},{8,10},{9,11},{10,... | collective-permute-start | bytes 786440 | tf_op jit(solution)/shard_map/ppermute | solution.py:133
  476.6 23.5 %collective-permute-start.23 = (bf16[128,1024]{1,0:T(8,128)(2,1)S(1)}, bf16[128,1024]{1,0:T(8,128)(2,1)S(1)}, u32[]{:S(2)}, u32[]{:S(2)}) collective-permute-start(bf16[128,1024]{1,0:T(8,128)(2,1)S(1)} %get-tuple-element.39), channel_id=1, source_target_pairs={{0,1},{1,2},{2,3},{3,0},{4,5},{5,6},{6,7},{7,4},{8,9},{9,10},{10,1... | collective-permute-start | bytes 786440 | tf_op jit(solution)/shard_map/ppermute | solution.py:133
  596.9 34.5 %copy-start.1 = (bf16[256,4096]{1,0:T(8,128)(2,1)S(1)}, bf16[256,4096]{1,0:T(8,128)(2,1)}, u32[]{:S(2)}) copy-start(bf16[256,4096]{1,0:T(8,128)(2,1)} %param.26) | copy-start | bytes 6291460
  (31 other events, 119.0 us)
Sparse Core Ops, SparseCore 0:
  41.6 51.7 all-gather.9
  95.9 46.6 all-gather.11
  144.5 45.5 all-gather.13
  306.0 54.1 reduce-scatter.3
  363.3 52.6 reduce-scatter.5
  419.4 52.6 reduce-scatter.7
  476.0 60.3 all-gather.21
  538.9 27.0 all-gather.15
  568.7 28.1 all-gather.17
  599.4 27.8 all-gather.19
